TPU v7x, 32 devices: a whole 2x2x4 slice. The times are simulated.
32 devices in a mesh: group: 2 (over y), frame: 4 (over z), row: 2 (over x), head: 2 (over core).
Axes of the slice: x: 2, y: 2, z: 4, core: 2. Of those that a mesh axis runs over, the one named last changes fastest.
Arguments:
- q_video: bfloat16 [16, 16, 16, 1536], P(('group', 'frame'), 'row', None, 'head'), parts along dimension 0, may hold values from -16 to 16
- k_video: bfloat16 [16, 16, 16, 1536], P(('group', 'frame'), 'row', None, 'head'), parts along dimension 0, may hold values from -8 to 8
- v_video: bfloat16 [16, 16, 16, 1536], P(('group', 'frame'), 'row', None, 'head'), parts along dimension 0, may hold values from -6 to 6
- q_reg: bfloat16 [256, 1536], P('group', 'head'), parts along dimension 0, may hold values from -16 to 16
- k_reg: bfloat16 [256, 1536], P('group', 'head'), parts along dimension 0, may hold values from -6 to 6
- v_reg: bfloat16 [256, 1536], P('group', 'head'), parts along dimension 0, may hold values from -6 to 6
- nbr_mask: int32 [4, 2, 2, 26], P('frame', 'row'), may hold values 0 or 1
Outputs:
- out_video: bfloat16 [16, 16, 16, 1536], P(('group', 'frame'), 'row', None, 'head'), parts along dimension 0
- out_reg: bfloat16 [256, 1536], P(('group', 'frame', 'row'), 'head'), parts along dimension 0
There are 2 independent parts, one for each index of `group`. A program takes and returns all parts, laid end to end along the dimension named above; an argument that names none is the same for every part. Nothing has to cross between parts.
All inputs are finite; a program needn't handle non-finite values. No bound on the sum of `nbr_mask` on one device may be relied on, other than what follows from the above.
Results may differ from a plain program's by a relative error of at most 0.0049.
Values may be sent and summed in bfloat16 or wider, within the bound.
A program may use at most 64 MiB of HBM per device.

v0:
```python
import jax
import jax.numpy as jnp
from jax import lax
from jax.sharding import PartitionSpec as P

HEAD_DIM = 128


def with_halo(array, sides, width):
    for axis, dim in sides:
        peers, length = (lax.axis_size(axis), array.shape[dim])
        up = [(i, (i + 1) % peers) for i in range(peers - 1)]
        down = [(j, i) for i, j in up]
        last = lax.slice_in_dim(array, length - width, length, axis=dim)
        first = lax.slice_in_dim(array, 0, width, axis=dim)
        before = lax.ppermute(last, axis, up)
        after = lax.ppermute(first, axis, down)
        array = jnp.concatenate([before, array, after], axis=dim)
    return array


def exact_product(weights, values):
    leading = weights.astype(values.dtype)
    remainder = (weights - leading.astype(weights.dtype)).astype(values.dtype)
    first = jnp.dot(leading, values, preferred_element_type=weights.dtype)
    return first + jnp.dot(remainder, values, preferred_element_type=weights.dtype)


def partial_softmax(query_rows, key_rows, value_rows, head_index, score_scale):
    query_head = lax.dynamic_slice_in_dim(query_rows, head_index * HEAD_DIM, HEAD_DIM, 1)
    key_head = lax.dynamic_slice_in_dim(key_rows, head_index * HEAD_DIM, HEAD_DIM, 1)
    value_head = lax.dynamic_slice_in_dim(value_rows, head_index * HEAD_DIM, HEAD_DIM, 1)
    scores = jnp.dot(query_head, key_head.T, preferred_element_type=jnp.float32) * score_scale
    row_max = jnp.max(scores, axis=-1)
    weights = jnp.exp(scores - row_max[:, None])
    weighted = exact_product(weights, value_head)
    return (row_max, jnp.sum(weights, axis=-1), weighted)


def per_head(query_rows, key_rows, value_rows, heads_dev, score_scale):

    def one_head(head_index):
        return partial_softmax(query_rows, key_rows, value_rows, head_index, score_scale)

    row_max, totals, weighted = lax.map(one_head, jnp.arange(heads_dev, dtype=jnp.int32))
    row_count = weighted.shape[1]
    return (
        row_max.T,
        totals.T,
        weighted.transpose(1, 0, 2).reshape(row_count, heads_dev * HEAD_DIM),
    )


def rescale(weighted, factor):
    row_count, heads_dev = factor.shape
    return (weighted.reshape(row_count, heads_dev, HEAD_DIM) * factor[:, :, None]).reshape(
        row_count, heads_dev * HEAD_DIM
    )


def combine(earlier, later):
    max_a, total_a, weighted_a = earlier
    max_b, total_b, weighted_b = later
    joint_max = jnp.maximum(max_a, max_b)
    factor_a = jnp.exp(max_a - joint_max)
    factor_b = jnp.exp(max_b - joint_max)
    return (
        joint_max,
        total_a * factor_a + total_b * factor_b,
        rescale(weighted_a, factor_a) + rescale(weighted_b, factor_b),
    )


def on_device(q_video, k_video, v_video, q_reg, k_reg, v_reg, nbr_mask):
    tile_f, tile_r, columns, features = q_video.shape
    col_tiles = nbr_mask.shape[2]
    tile_c = columns // col_tiles
    tile_size = tile_f * tile_r * tile_c
    heads_dev = features // HEAD_DIM
    registers = q_reg.shape[0]
    score_scale = HEAD_DIM ** (-0.5)
    frame_count = lax.axis_size("frame")
    rowdev_count = lax.axis_size("row")
    frame_pos = lax.axis_index("frame")
    rowdev_pos = lax.axis_index("row")
    paired = jnp.stack([k_video, v_video], 0)[None, None]
    near_block = with_halo(paired, (("frame", 0), ("row", 1)), 1)
    local_part = per_head(
        q_reg, k_video.reshape(-1, features), v_video.reshape(-1, features), heads_dev, score_scale
    )
    local_max, local_total, local_weighted = local_part
    row_share = registers // (frame_count * rowdev_count)
    row_start = (frame_pos * rowdev_count + rowdev_pos) * row_share
    own_queries = lax.dynamic_slice_in_dim(q_reg, row_start, row_share, 0)
    self_part = per_head(own_queries, k_reg, v_reg, heads_dev, score_scale)

    def own_rows(array):
        return lax.dynamic_slice_in_dim(array, row_start, row_share, 0)

    global_max = lax.pmax(local_max, ("frame", "row"))
    factor = jnp.exp(local_max - global_max)
    reduced = lax.psum((rescale(local_weighted, factor), local_total * factor), ("frame", "row"))
    collected = (own_rows(global_max), own_rows(reduced[1]), own_rows(reduced[0]))
    final_max, final_total, final_weighted = combine(collected, self_part)
    out_reg = (
        (final_weighted.reshape(row_share, heads_dev, HEAD_DIM) / final_total[:, :, None])
        .reshape(row_share, features)
        .astype(jnp.bfloat16)
    )
    near_block = near_block.reshape(3, 3, 2, tile_f, tile_r, col_tiles, tile_c, features)
    queries = (
        q_video.reshape(tile_f, tile_r, col_tiles, tile_c, features)
        .transpose(2, 0, 1, 3, 4)
        .reshape(col_tiles, tile_size, features)
    )
    window = min(3, col_tiles)
    full_mask = jnp.concatenate(
        [nbr_mask[0, 0, :, :13], jnp.ones((col_tiles, 1), jnp.int32), nbr_mask[0, 0, :, 13:]], 1
    )
    offsets = jnp.arange(3, dtype=jnp.int32) - 1
    frame_inside = (frame_pos + offsets >= 0) & (frame_pos + offsets < frame_count)
    row_inside = (rowdev_pos + offsets >= 0) & (rowdev_pos + offsets < rowdev_count)

    def one_item(item_index):
        col_index = item_index // heads_dev
        head_index = item_index % heads_dev
        first_col = jnp.clip(col_index - 1, 0, col_tiles - window)
        anchor = jnp.zeros((), jnp.int32)
        near_piece = lax.dynamic_slice(
            near_block,
            (anchor, anchor, anchor, anchor, anchor, first_col, anchor, head_index * HEAD_DIM),
            (3, 3, 2, tile_f, tile_r, window, tile_c, HEAD_DIM),
        )
        near_head = near_piece.transpose(2, 0, 1, 5, 3, 4, 6, 7).reshape(
            2, 3, 3, window, tile_size, HEAD_DIM
        )
        key_cols = first_col + jnp.arange(window, dtype=jnp.int32)
        offset_codes = (
            (offsets[:, None, None] + 1) * 9
            + (offsets[None, :, None] + 1) * 3
            + (key_cols - col_index + 1)[None, None, :]
        )
        mask_row = lax.dynamic_index_in_dim(full_mask, col_index, 0, keepdims=False)
        picked = jnp.sum(
            jnp.where(offset_codes[..., None] == jnp.arange(27, dtype=jnp.int32), mask_row, 0),
            axis=-1,
        )
        adjacent = jnp.abs(key_cols - col_index) <= 1
        allowed = (
            (picked == 1)
            & frame_inside[:, None, None]
            & row_inside[None, :, None]
            & adjacent[None, None, :]
        )
        key_ok = jnp.concatenate(
            [
                jnp.repeat(
                    allowed.reshape(-1), tile_size, total_repeat_length=9 * window * tile_size
                ),
                jnp.ones((registers,), bool),
            ]
        )
        key_rows = jnp.concatenate(
            [
                near_head[0].reshape(-1, HEAD_DIM),
                lax.dynamic_slice_in_dim(k_reg, head_index * HEAD_DIM, HEAD_DIM, 1),
            ],
            0,
        )
        value_rows = jnp.concatenate(
            [
                near_head[1].reshape(-1, HEAD_DIM),
                lax.dynamic_slice_in_dim(v_reg, head_index * HEAD_DIM, HEAD_DIM, 1),
            ],
            0,
        )
        query_head = lax.dynamic_slice(
            queries, (col_index, anchor, head_index * HEAD_DIM), (1, tile_size, HEAD_DIM)
        )[0]
        scores = jnp.dot(query_head, key_rows.T, preferred_element_type=jnp.float32) * score_scale
        scores = jnp.where(key_ok[None, :], scores, -jnp.inf)
        weights = jax.nn.softmax(scores, axis=-1).astype(jnp.bfloat16)
        return jnp.dot(weights, value_rows, preferred_element_type=jnp.float32).astype(jnp.bfloat16)

    results = lax.map(one_item, jnp.arange(col_tiles * heads_dev, dtype=jnp.int32))
    out_video = (
        results.reshape(col_tiles, heads_dev, tile_f, tile_r, tile_c, HEAD_DIM)
        .transpose(2, 3, 0, 4, 1, 5)
        .reshape(tile_f, tile_r, columns, features)
    )
    return (out_video, out_reg)


def solution(mesh):
    return jax.shard_map(
        on_device,
        mesh=mesh,
        in_specs=(
            P(("group", "frame"), "row", None, "head"),
            P(("group", "frame"), "row", None, "head"),
            P(("group", "frame"), "row", None, "head"),
            P("group", "head"),
            P("group", "head"),
            P("group", "head"),
            P("frame", "row", None, None),
        ),
        out_specs=(
            P(("group", "frame"), "row", None, "head"),
            P(("group", "frame", "row"), "head"),
        ),
        check_vma=False,
    )
```

profile of v0, /device:TPU:0, one launch (start us, length us, event | category | flops | bytes accessed | tf_op | source)
XLA Modules:
  0.0 386.3 jit_solution(3703701731983514804)
XLA Ops:
  8.4 5.0 %collective-permute-start = (bf16[1,1,2,2,8,16,768]{6,5,4,3,2,1,0:T(8,128)(2,1)S(1)}, bf16[1,1,2,2,8,16,768]{6,5,4,3,2,1,0:T(8,128)(2,1)S(1)}, u32[]{:S(2)}, u32[]{:S(2)}) collective-permute-start(bf16[1,1,2,2,8,16,768]{6,5,4,3,2,1,0:T(8,128)(2,1)S(1)} %maximum_bitcast_fusion.1), channel_id=1, source_target_pairs={{0,4},{4,8},{8,12},{1,5},{5,9},{9,13},{2,6},{6,10},{10,14},{3,7},{... | collective-permute-start | bytes 2359304 | tf_op jit(solution)/shard_map/ppermute | solution.py:16
  13.4 1.3 collective-permute-start.1
  14.7 29.3 %while.46 = (s32[]{:T(128)}, f32[6,128]{1,0:T(8,128)S(1)}, f32[6,128]{1,0:T(8,128)S(1)}, f32[6,128,128]{1,2,0:T(8,128)S(1)}, s32[6]{0:T(128)S(1)}, /*index=5*/bf...) while((s32[]{:T(128)}, f32[6,128]{1,0:T(8,128)S(1)}, ...), condition=%wide.region_8.9_spmd, body=%wide.region_5.0_spmd.sunk | while | flops 25542404 | bytes 1218243 | solution.py:45
  44.0 22.7 %pmax.7 = f32[128,6]{0,1:T(8,128)S(1)} all-reduce(f32[128,6]{0,1:T(8,128)S(1)} %bitcast.239), channel_id=1, replica_groups=mesh['group'=2,'frame'=4,'row'=2,'head'=2] {'frame','row'}, use_global_device_ids=true, to_apply=%region_9.10 | all-reduce | flops 768 | bytes 6144 | tf_op jit(solution)/shard_map/pmax | solution.py:100
  68.6 1.7 pad_maximum_fusion
  70.2 2.8 collective-permute-start.2
  73.1 1.3 collective-permute-start.3
  74.4 17.6 %while.47 = (s32[]{:T(128)}, f32[6,16]{1,0:T(8,128)S(1)}, f32[6,16]{1,0:T(8,128)S(1)}, f32[6,16,128]{2,1,0:T(8,128)S(1)}, s32[6]{0:T(128)S(1)}, /*index=5*/bf16[...) while((s32[]{:T(128)}, f32[6,16]{1,0:T(8,128)S(1)}, ...), condition=%wide.region_14.15_spmd, body=%wide.region_11.14_spmd.sunk | while | flops 1597414 | bytes 162435 | solution.py:45
  92.0 43.7 %psum.15 = f32[128,6]{0,1:T(8,128)S(1)} all-reduce(f32[128,6]{0,1:T(8,128)S(1)} %get-tuple-element.582), channel_id=1, replica_groups=mesh['group'=2,'frame'=4,'row'=2,'head'=2] {'frame','row'}, use_global_device_ids=true, to_apply=%region_15.16 | all-reduce | flops 768 | bytes 6144 | tf_op jit(solution)/shard_map/psum | solution.py:102
  137.6 1.5 fusion.61
  139.1 5.9 %maximum_bitcast_fusion = bf16[3,3,2,2,8,2,8,768]{7,6,5,4,3,2,1,0:T(8,128)(2,1)} fusion(bf16[3,1,2,2,8,16,768]{6,5,4,3,2,1,0:T(8,128)(2,1)} %collective-permute-done.3, bf16[1,1,2,2,8,16,768]{6,5,4,3,2,1,0:T(8,128)(2,1)S(1)} %collective-permute-done.1, bf16[1,1,2,2,8,16,768]{6,5,4,3,2,1,0:T(8,128)(2,1)S(1)} %maximum_bitcast_fusion.1, ...), kind=kLoop, calls=%fused_computation.100 | loop fusion | flops 14155776 | bytes 14155776 | tf_op jit(solution)/shard_map/reshape | solution.py:110
  145.0 233.7 %while.48 = (s32[]{:T(128)}, bf16[12,128,128]{2,1,0:T(8,128)(2,1)S(1)}, s32[12]{0:T(128)S(1)}, s32[2,27]{1,0:T(2,128)S(1)}, bf16[2,128,768]{2,1,0:T(8,128)(2,1)S...) while((s32[]{:T(128)}, ...), condition=%wide.region_4.5_spmd.clone, body=%wide.region_0.4_spmd.clone.sunk | while | flops 164492608 | bytes 10002113 | solution.py:185
  149.0 4.7 %select_reduce_fusion.2 = (pred[2304]{0:T(1024)(128)(4,1)S(1)}, pred[2304]{0:T(1024)(128)(4,1)S(1)}, pred[2304]{0:T(1024)(128)(4,1)S(1)}, pred[2304]{0:T(1024)(1...) fusion(pred[]{:T(512)} %bitcast.204, ...), kind=kLoop, calls=%fused_computation.55.clone.1 | loop fusion | flops 57600 | bytes 46087 | tf_op jit(solution)/shard_map/while/body/eval_jaxpr/jit(_take)/gather | solution.py:157
  153.7 7.0 %fusion.121 = pred[2304]{0:T(1024)(128)(4,1)S(1)} fusion(pred[2304]{0:T(1024)(128)(4,1)S(1)} %get-tuple-element.846, pred[2304]{0:T(1024)(128)(4,1)S(1)} %get-tuple-element.847, pred[2304]{0:T(1024)(128)(4,1)S(1)} %get-tuple-element.848, pred[2304]{0:T(1024)(128)(4,1)S(1)} %get-tuple-element.849, pred[2304]{0:T(1024)(128)(4,1)S(1)} %get-tuple-element.850, ...), kind=kLoop, calls=%fused_computation.79.clone.1 | loop fusion | flops 46080 | bytes 29963 | tf_op jit(solution)/shard_map/while/body/eval_jaxpr/jit(_take)/select_n | solution.py:157
  161.5 1.6 copy_bitcast_fusion.3
  168.5 4.7 %select_reduce_fusion.2 = (pred[2304]{0:T(1024)(128)(4,1)S(1)}, pred[2304]{0:T(1024)(128)(4,1)S(1)}, pred[2304]{0:T(1024)(128)(4,1)S(1)}, pred[2304]{0:T(1024)(1...) fusion(pred[]{:T(512)} %bitcast.204, ...), kind=kLoop, calls=%fused_computation.55.clone.1 | loop fusion | flops 57600 | bytes 46087 | tf_op jit(solution)/shard_map/while/body/eval_jaxpr/jit(_take)/gather | solution.py:157
  173.2 7.0 %fusion.121 = pred[2304]{0:T(1024)(128)(4,1)S(1)} fusion(pred[2304]{0:T(1024)(128)(4,1)S(1)} %get-tuple-element.846, pred[2304]{0:T(1024)(128)(4,1)S(1)} %get-tuple-element.847, pred[2304]{0:T(1024)(128)(4,1)S(1)} %get-tuple-element.848, pred[2304]{0:T(1024)(128)(4,1)S(1)} %get-tuple-element.849, pred[2304]{0:T(1024)(128)(4,1)S(1)} %get-tuple-element.850, ...), kind=kLoop, calls=%fused_computation.79.clone.1 | loop fusion | flops 46080 | bytes 29963 | tf_op jit(solution)/shard_map/while/body/eval_jaxpr/jit(_take)/select_n | solution.py:157
  181.0 1.6 copy_bitcast_fusion.3
  187.9 4.7 %select_reduce_fusion.2 = (pred[2304]{0:T(1024)(128)(4,1)S(1)}, pred[2304]{0:T(1024)(128)(4,1)S(1)}, pred[2304]{0:T(1024)(128)(4,1)S(1)}, pred[2304]{0:T(1024)(1...) fusion(pred[]{:T(512)} %bitcast.204, ...), kind=kLoop, calls=%fused_computation.55.clone.1 | loop fusion | flops 57600 | bytes 46087 | tf_op jit(solution)/shard_map/while/body/eval_jaxpr/jit(_take)/gather | solution.py:157
  192.6 7.0 %fusion.121 = pred[2304]{0:T(1024)(128)(4,1)S(1)} fusion(pred[2304]{0:T(1024)(128)(4,1)S(1)} %get-tuple-element.846, pred[2304]{0:T(1024)(128)(4,1)S(1)} %get-tuple-element.847, pred[2304]{0:T(1024)(128)(4,1)S(1)} %get-tuple-element.848, pred[2304]{0:T(1024)(128)(4,1)S(1)} %get-tuple-element.849, pred[2304]{0:T(1024)(128)(4,1)S(1)} %get-tuple-element.850, ...), kind=kLoop, calls=%fused_computation.79.clone.1 | loop fusion | flops 46080 | bytes 29963 | tf_op jit(solution)/shard_map/while/body/eval_jaxpr/jit(_take)/select_n | solution.py:157
  200.4 1.6 copy_bitcast_fusion.3
  207.4 4.7 %select_reduce_fusion.2 = (pred[2304]{0:T(1024)(128)(4,1)S(1)}, pred[2304]{0:T(1024)(128)(4,1)S(1)}, pred[2304]{0:T(1024)(128)(4,1)S(1)}, pred[2304]{0:T(1024)(1...) fusion(pred[]{:T(512)} %bitcast.204, ...), kind=kLoop, calls=%fused_computation.55.clone.1 | loop fusion | flops 57600 | bytes 46087 | tf_op jit(solution)/shard_map/while/body/eval_jaxpr/jit(_take)/gather | solution.py:157
  212.1 7.0 %fusion.121 = pred[2304]{0:T(1024)(128)(4,1)S(1)} fusion(pred[2304]{0:T(1024)(128)(4,1)S(1)} %get-tuple-element.846, pred[2304]{0:T(1024)(128)(4,1)S(1)} %get-tuple-element.847, pred[2304]{0:T(1024)(128)(4,1)S(1)} %get-tuple-element.848, pred[2304]{0:T(1024)(128)(4,1)S(1)} %get-tuple-element.849, pred[2304]{0:T(1024)(128)(4,1)S(1)} %get-tuple-element.850, ...), kind=kLoop, calls=%fused_computation.79.clone.1 | loop fusion | flops 46080 | bytes 29963 | tf_op jit(solution)/shard_map/while/body/eval_jaxpr/jit(_take)/select_n | solution.py:157
  219.9 1.6 copy_bitcast_fusion.3
  226.9 4.7 %select_reduce_fusion.2 = (pred[2304]{0:T(1024)(128)(4,1)S(1)}, pred[2304]{0:T(1024)(128)(4,1)S(1)}, pred[2304]{0:T(1024)(128)(4,1)S(1)}, pred[2304]{0:T(1024)(1...) fusion(pred[]{:T(512)} %bitcast.204, ...), kind=kLoop, calls=%fused_computation.55.clone.1 | loop fusion | flops 57600 | bytes 46087 | tf_op jit(solution)/shard_map/while/body/eval_jaxpr/jit(_take)/gather | solution.py:157
  231.6 7.0 %fusion.121 = pred[2304]{0:T(1024)(128)(4,1)S(1)} fusion(pred[2304]{0:T(1024)(128)(4,1)S(1)} %get-tuple-element.846, pred[2304]{0:T(1024)(128)(4,1)S(1)} %get-tuple-element.847, pred[2304]{0:T(1024)(128)(4,1)S(1)} %get-tuple-element.848, pred[2304]{0:T(1024)(128)(4,1)S(1)} %get-tuple-element.849, pred[2304]{0:T(1024)(128)(4,1)S(1)} %get-tuple-element.850, ...), kind=kLoop, calls=%fused_computation.79.clone.1 | loop fusion | flops 46080 | bytes 29963 | tf_op jit(solution)/shard_map/while/body/eval_jaxpr/jit(_take)/select_n | solution.py:157
  239.4 1.6 copy_bitcast_fusion.3
  246.4 4.7 %select_reduce_fusion.2 = (pred[2304]{0:T(1024)(128)(4,1)S(1)}, pred[2304]{0:T(1024)(128)(4,1)S(1)}, pred[2304]{0:T(1024)(128)(4,1)S(1)}, pred[2304]{0:T(1024)(1...) fusion(pred[]{:T(512)} %bitcast.204, ...), kind=kLoop, calls=%fused_computation.55.clone.1 | loop fusion | flops 57600 | bytes 46087 | tf_op jit(solution)/shard_map/while/body/eval_jaxpr/jit(_take)/gather | solution.py:157
  251.1 7.0 %fusion.121 = pred[2304]{0:T(1024)(128)(4,1)S(1)} fusion(pred[2304]{0:T(1024)(128)(4,1)S(1)} %get-tuple-element.846, pred[2304]{0:T(1024)(128)(4,1)S(1)} %get-tuple-element.847, pred[2304]{0:T(1024)(128)(4,1)S(1)} %get-tuple-element.848, pred[2304]{0:T(1024)(128)(4,1)S(1)} %get-tuple-element.849, pred[2304]{0:T(1024)(128)(4,1)S(1)} %get-tuple-element.850, ...), kind=kLoop, calls=%fused_computation.79.clone.1 | loop fusion | flops 46080 | bytes 29963 | tf_op jit(solution)/shard_map/while/body/eval_jaxpr/jit(_take)/select_n | solution.py:157
  258.9 1.6 copy_bitcast_fusion.3
  265.8 4.7 %select_reduce_fusion.2 = (pred[2304]{0:T(1024)(128)(4,1)S(1)}, pred[2304]{0:T(1024)(128)(4,1)S(1)}, pred[2304]{0:T(1024)(128)(4,1)S(1)}, pred[2304]{0:T(1024)(1...) fusion(pred[]{:T(512)} %bitcast.204, ...), kind=kLoop, calls=%fused_computation.55.clone.1 | loop fusion | flops 57600 | bytes 46087 | tf_op jit(solution)/shard_map/while/body/eval_jaxpr/jit(_take)/gather | solution.py:157
  270.5 7.0 %fusion.121 = pred[2304]{0:T(1024)(128)(4,1)S(1)} fusion(pred[2304]{0:T(1024)(128)(4,1)S(1)} %get-tuple-element.846, pred[2304]{0:T(1024)(128)(4,1)S(1)} %get-tuple-element.847, pred[2304]{0:T(1024)(128)(4,1)S(1)} %get-tuple-element.848, pred[2304]{0:T(1024)(128)(4,1)S(1)} %get-tuple-element.849, pred[2304]{0:T(1024)(128)(4,1)S(1)} %get-tuple-element.850, ...), kind=kLoop, calls=%fused_computation.79.clone.1 | loop fusion | flops 46080 | bytes 29963 | tf_op jit(solution)/shard_map/while/body/eval_jaxpr/jit(_take)/select_n | solution.py:157
  278.4 1.6 copy_bitcast_fusion.3
  285.3 4.7 %select_reduce_fusion.2 = (pred[2304]{0:T(1024)(128)(4,1)S(1)}, pred[2304]{0:T(1024)(128)(4,1)S(1)}, pred[2304]{0:T(1024)(128)(4,1)S(1)}, pred[2304]{0:T(1024)(1...) fusion(pred[]{:T(512)} %bitcast.204, ...), kind=kLoop, calls=%fused_computation.55.clone.1 | loop fusion | flops 57600 | bytes 46087 | tf_op jit(solution)/shard_map/while/body/eval_jaxpr/jit(_take)/gather | solution.py:157
  290.0 7.0 %fusion.121 = pred[2304]{0:T(1024)(128)(4,1)S(1)} fusion(pred[2304]{0:T(1024)(128)(4,1)S(1)} %get-tuple-element.846, pred[2304]{0:T(1024)(128)(4,1)S(1)} %get-tuple-element.847, pred[2304]{0:T(1024)(128)(4,1)S(1)} %get-tuple-element.848, pred[2304]{0:T(1024)(128)(4,1)S(1)} %get-tuple-element.849, pred[2304]{0:T(1024)(128)(4,1)S(1)} %get-tuple-element.850, ...), kind=kLoop, calls=%fused_computation.79.clone.1 | loop fusion | flops 46080 | bytes 29963 | tf_op jit(solution)/shard_map/while/body/eval_jaxpr/jit(_take)/select_n | solution.py:157
  297.8 1.6 copy_bitcast_fusion.3
  304.8 4.7 %select_reduce_fusion.2 = (pred[2304]{0:T(1024)(128)(4,1)S(1)}, pred[2304]{0:T(1024)(128)(4,1)S(1)}, pred[2304]{0:T(1024)(128)(4,1)S(1)}, pred[2304]{0:T(1024)(1...) fusion(pred[]{:T(512)} %bitcast.204, ...), kind=kLoop, calls=%fused_computation.55.clone.1 | loop fusion | flops 57600 | bytes 46087 | tf_op jit(solution)/shard_map/while/body/eval_jaxpr/jit(_take)/gather | solution.py:157
  309.5 7.0 %fusion.121 = pred[2304]{0:T(1024)(128)(4,1)S(1)} fusion(pred[2304]{0:T(1024)(128)(4,1)S(1)} %get-tuple-element.846, pred[2304]{0:T(1024)(128)(4,1)S(1)} %get-tuple-element.847, pred[2304]{0:T(1024)(128)(4,1)S(1)} %get-tuple-element.848, pred[2304]{0:T(1024)(128)(4,1)S(1)} %get-tuple-element.849, pred[2304]{0:T(1024)(128)(4,1)S(1)} %get-tuple-element.850, ...), kind=kLoop, calls=%fused_computation.79.clone.1 | loop fusion | flops 46080 | bytes 29963 | tf_op jit(solution)/shard_map/while/body/eval_jaxpr/jit(_take)/select_n | solution.py:157
  317.3 1.6 copy_bitcast_fusion.3
  324.3 4.7 %select_reduce_fusion.2 = (pred[2304]{0:T(1024)(128)(4,1)S(1)}, pred[2304]{0:T(1024)(128)(4,1)S(1)}, pred[2304]{0:T(1024)(128)(4,1)S(1)}, pred[2304]{0:T(1024)(1...) fusion(pred[]{:T(512)} %bitcast.204, ...), kind=kLoop, calls=%fused_computation.55.clone.1 | loop fusion | flops 57600 | bytes 46087 | tf_op jit(solution)/shard_map/while/body/eval_jaxpr/jit(_take)/gather | solution.py:157
  329.0 7.0 %fusion.121 = pred[2304]{0:T(1024)(128)(4,1)S(1)} fusion(pred[2304]{0:T(1024)(128)(4,1)S(1)} %get-tuple-element.846, pred[2304]{0:T(1024)(128)(4,1)S(1)} %get-tuple-element.847, pred[2304]{0:T(1024)(128)(4,1)S(1)} %get-tuple-element.848, pred[2304]{0:T(1024)(128)(4,1)S(1)} %get-tuple-element.849, pred[2304]{0:T(1024)(128)(4,1)S(1)} %get-tuple-element.850, ...), kind=kLoop, calls=%fused_computation.79.clone.1 | loop fusion | flops 46080 | bytes 29963 | tf_op jit(solution)/shard_map/while/body/eval_jaxpr/jit(_take)/select_n | solution.py:157
  336.8 1.6 copy_bitcast_fusion.3
  343.7 4.7 %select_reduce_fusion.2 = (pred[2304]{0:T(1024)(128)(4,1)S(1)}, pred[2304]{0:T(1024)(128)(4,1)S(1)}, pred[2304]{0:T(1024)(128)(4,1)S(1)}, pred[2304]{0:T(1024)(1...) fusion(pred[]{:T(512)} %bitcast.204, ...), kind=kLoop, calls=%fused_computation.55.clone.1 | loop fusion | flops 57600 | bytes 46087 | tf_op jit(solution)/shard_map/while/body/eval_jaxpr/jit(_take)/gather | solution.py:157
  348.4 7.0 %fusion.121 = pred[2304]{0:T(1024)(128)(4,1)S(1)} fusion(pred[2304]{0:T(1024)(128)(4,1)S(1)} %get-tuple-element.846, pred[2304]{0:T(1024)(128)(4,1)S(1)} %get-tuple-element.847, pred[2304]{0:T(1024)(128)(4,1)S(1)} %get-tuple-element.848, pred[2304]{0:T(1024)(128)(4,1)S(1)} %get-tuple-element.849, pred[2304]{0:T(1024)(128)(4,1)S(1)} %get-tuple-element.850, ...), kind=kLoop, calls=%fused_computation.79.clone.1 | loop fusion | flops 46080 | bytes 29963 | tf_op jit(solution)/shard_map/while/body/eval_jaxpr/jit(_take)/select_n | solution.py:157
  356.3 1.6 copy_bitcast_fusion.3
  363.2 4.7 %select_reduce_fusion.2 = (pred[2304]{0:T(1024)(128)(4,1)S(1)}, pred[2304]{0:T(1024)(128)(4,1)S(1)}, pred[2304]{0:T(1024)(128)(4,1)S(1)}, pred[2304]{0:T(1024)(1...) fusion(pred[]{:T(512)} %bitcast.204, ...), kind=kLoop, calls=%fused_computation.55.clone.1 | loop fusion | flops 57600 | bytes 46087 | tf_op jit(solution)/shard_map/while/body/eval_jaxpr/jit(_take)/gather | solution.py:157
  367.9 7.0 %fusion.121 = pred[2304]{0:T(1024)(128)(4,1)S(1)} fusion(pred[2304]{0:T(1024)(128)(4,1)S(1)} %get-tuple-element.846, pred[2304]{0:T(1024)(128)(4,1)S(1)} %get-tuple-element.847, pred[2304]{0:T(1024)(128)(4,1)S(1)} %get-tuple-element.848, pred[2304]{0:T(1024)(128)(4,1)S(1)} %get-tuple-element.849, pred[2304]{0:T(1024)(128)(4,1)S(1)} %get-tuple-element.850, ...), kind=kLoop, calls=%fused_computation.79.clone.1 | loop fusion | flops 46080 | bytes 29963 | tf_op jit(solution)/shard_map/while/body/eval_jaxpr/jit(_take)/select_n | solution.py:157
  375.7 1.6 copy_bitcast_fusion.3
  (364 shorter events, 93.6 us)
Async XLA Ops:
  7.2 130.2 %all-reduce.3.cloned.1.call-start = ((), (), s32[]{:S(2)}) async-start(), calls=%async_computation | async-start | bytes 786432 | tf_op jit(solution)/shard_map/psum | solution.py:102
  8.4 60.2 %collective-permute-start = (bf16[1,1,2,2,8,16,768]{6,5,4,3,2,1,0:T(8,128)(2,1)S(1)}, bf16[1,1,2,2,8,16,768]{6,5,4,3,2,1,0:T(8,128)(2,1)S(1)}, u32[]{:S(2)}, u32[]{:S(2)}) collective-permute-start(bf16[1,1,2,2,8,16,768]{6,5,4,3,2,1,0:T(8,128)(2,1)S(1)} %maximum_bitcast_fusion.1), channel_id=1, source_target_pairs={{0,4},{4,8},{8,12},{1,5},{5,9},{9,13},{2,6},{6,10},{10,14},{3,7},{... | collective-permute-start | bytes 2359304 | tf_op jit(solution)/shard_map/ppermute | solution.py:16
  13.4 55.2 %collective-permute-start.1 = (bf16[1,1,2,2,8,16,768]{6,5,4,3,2,1,0:T(8,128)(2,1)S(1)}, bf16[1,1,2,2,8,16,768]{6,5,4,3,2,1,0:T(8,128)(2,1)S(1)}, u32[]{:S(2)}, u32[]{:S(2)}) collective-permute-start(bf16[1,1,2,2,8,16,768]{6,5,4,3,2,1,0:T(8,128)(2,1)S(1)} %maximum_bitcast_fusion.1), channel_id=1, source_target_pairs={{4,0},{8,4},{12,8},{5,1},{9,5},{13,9},{6,2},{10,6},{14,10},{7,3},{... | collective-permute-start | bytes 2359304 | tf_op jit(solution)/shard_map/ppermute | solution.py:17
  68.5 5.8 %copy-start.2 = (bf16[128,768]{1,0:T(8,128)(2,1)S(1)}, bf16[128,768]{1,0:T(8,128)(2,1)}, u32[]{:S(2)}) copy-start(bf16[128,768]{1,0:T(8,128)(2,1)} %param.20) | copy-start | bytes 589828
  68.6 67.5 %copy-start = (bf16[2,8,16,768]{3,2,1,0:T(8,128)(2,1)S(1)}, bf16[2,8,16,768]{3,2,1,0:T(8,128)(2,1)}, u32[]{:S(2)}) copy-start(bf16[2,8,16,768]{3,2,1,0:T(8,128)(2,1)} %param.15) | copy-start | bytes 1179652
  70.2 65.8 %copy-start.3 = (s32[1,1,2,26]{3,2,1,0:T(2,128)S(1)}, s32[1,1,2,26]{3,2,1,0:T(2,128)}, u32[]{:S(2)}) copy-start(s32[1,1,2,26]{3,2,1,0:T(2,128)} %param.21) | copy-start | bytes 628
  70.2 68.8 %collective-permute-start.2 = (bf16[3,1,2,2,8,16,768]{6,5,4,3,2,1,0:T(8,128)(2,1)}, bf16[3,1,2,2,8,16,768]{6,5,4,3,2,1,0:T(8,128)(2,1)}, u32[]{:S(2)}, u32[]{:S(2)}) collective-permute-start(bf16[3,1,2,2,8,16,768]{6,5,4,3,2,1,0:T(8,128)(2,1)} %pad_maximum_fusion), channel_id=1, source_target_pairs={{0,2},{1,3},{4,6},{5,7},{8,10},{9,11},{12,14},{13,15},{16,18},{17,... | collective-permute-start | bytes 7077896 | tf_op jit(solution)/shard_map/ppermute | solution.py:16
  73.1 66.0 %collective-permute-start.3 = (bf16[3,1,2,2,8,16,768]{6,5,4,3,2,1,0:T(8,128)(2,1)}, bf16[3,1,2,2,8,16,768]{6,5,4,3,2,1,0:T(8,128)(2,1)}, u32[]{:S(2)}, u32[]{:S(2)}) collective-permute-start(bf16[3,1,2,2,8,16,768]{6,5,4,3,2,1,0:T(8,128)(2,1)} %pad_maximum_fusion), channel_id=1, source_target_pairs={{2,0},{3,1},{6,4},{7,5},{10,8},{11,9},{14,12},{15,13},{18,16},{19,... | collective-permute-start | bytes 7077896 | tf_op jit(solution)/shard_map/ppermute | solution.py:17
  139.1 5.9 %copy-start.1 = (bf16[12,128,128]{2,1,0:T(8,128)(2,1)S(1)}, bf16[12,128,128]{2,1,0:T(8,128)(2,1)}, u32[]{:S(2)}) copy-start(bf16[12,128,128]{2,1,0:T(8,128)(2,1)} %custom-call.6) | copy-start | bytes 1179652
Sparse Core Ops, SparseCore 0:
  67.9 69.4 all-reduce.2
where the time goes:
time: 392 us; the launch traced here: 386 us
  other arithmetic  164 us (42%)
  blocking collectives  66.4 us (17%)
  local copies, waits for them, and re-layouts  58.4 us (15%)
  matrix products  38.3 us (10%)
  loops' own time  33.3 us (8%)
  between operations  14.2 us (4%)
  starting transfers between devices  10.4 us (3%)
    select_n x12, other arithmetic, one_item(): jnp.repeat(allowed.reshape(-1), tile_size, total_repeat_length=9 * window...  84.1 us
    gather x12, other arithmetic, one_item(): jnp.repeat(allowed.reshape(-1), tile_size, total_repeat_length=9 * window...  56.4 us
    psum x1, blocking collectives, on_device(): lax.psum((rescale(local_weighted, factor), local_total * factor), ('frame...  43.7 us
    another operation x1, loops' own time, on_device(): lax.map(one_item, jnp.arange(col_tiles * heads_dev, dtype=jnp.int32))  25 us
    pmax x1, blocking collectives, on_device(): global_max = lax.pmax(local_max, ('frame', 'row'))  22.7 us
    transpose x12, local copies, waits for them, and re-layouts, one_item(): near_piece.transpose(2, 0, 1, 5, 3, 4, 6, 7)  18.9 us
    dot_general x12, matrix products, partial_softmax(): jnp.dot(query_head, key_head.T, preferred_element_type=jnp.float32)  12.8 us
    dynamic_slice x12, local copies, waits for them, and re-layouts, one_item(): lax.dynamic_slice_in_dim(v_reg, head_index * HEAD_DIM, HEAD_DIM, 1)  9.27 us
  transfers between devices with their start and end apart: 5, of which 1 were waited for; matrix products, arithmetic and copies ran while one was open for 11% of the time, Pallas kernels for 0%

commit v1 on v0

--- a/solution.py
+++ b/solution.py
@@ -99,7 +99,9 @@
 
     global_max = lax.pmax(local_max, ("frame", "row"))
     factor = jnp.exp(local_max - global_max)
-    reduced = lax.psum((rescale(local_weighted, factor), local_total * factor), ("frame", "row"))
+    reduced = lax.psum(
+        lax.psum((rescale(local_weighted, factor), local_total * factor), "row"), "frame"
+    )
     collected = (own_rows(global_max), own_rows(reduced[1]), own_rows(reduced[0]))
     final_max, final_total, final_weighted = combine(collected, self_part)
     out_reg = (

time: 392 us -> 431 us (1.099)
  waiting for transfers between devices: 1.19 us -> 34.4 us
  blocking collectives: 66.4 us -> 72.4 us
    psum x1 -> x2, waiting for transfers between devices: 1.16 us -> 34.3 us  [the longest x1 34.3 us: on_device(): lax.psum(lax.psum((rescale(local_weighted, factor), local_total * factor)...]
    psum x1 -> x2, blocking collectives: 43.7 us -> 49.7 us  [the longest x1 39.7 us: on_device(): lax.psum((rescale(local_weighted, factor), local_total * factor), 'row')]
  transfers between devices with their start and end apart: 5 -> 6, of which waited for: 1 -> 1; matrix products, arithmetic and copies ran while one was open for 11% -> 10% of each run, Pallas kernels for 0% -> 0%
where the time goes in v1:
time: 431 us; the launch traced here: 425 us
  other arithmetic  164 us (38%)
  blocking collectives  72.4 us (17%)
  local copies, waits for them, and re-layouts  58.1 us (13%)
  matrix products  38.3 us (9%)
  waiting for transfers between devices  34.4 us (8%)
  loops' own time  33.3 us (8%)
  between operations  14.2 us (3%)
  starting transfers between devices  10.4 us (2%)
    select_n x12, other arithmetic, one_item(): jnp.repeat(allowed.reshape(-1), tile_size, total_repeat_length=9 * window...  84.1 us
    gather x12, other arithmetic, one_item(): jnp.repeat(allowed.reshape(-1), tile_size, total_repeat_length=9 * window...  56.4 us
    psum x1, blocking collectives, on_device(): lax.psum((rescale(local_weighted, factor), local_total * factor), 'row')  39.7 us
    psum x1, waiting for transfers between devices, on_device(): lax.psum(lax.psum((rescale(local_weighted, factor), local_total * factor)...  34.3 us
    another operation x1, loops' own time, on_device(): lax.map(one_item, jnp.arange(col_tiles * heads_dev, dtype=jnp.int32))  25 us
    pmax x1, blocking collectives, on_device(): global_max = lax.pmax(local_max, ('frame', 'row'))  22.7 us
    transpose x12, local copies, waits for them, and re-layouts, one_item(): near_piece.transpose(2, 0, 1, 5, 3, 4, 6, 7)  18.9 us
    dot_general x12, matrix products, partial_softmax(): jnp.dot(query_head, key_head.T, preferred_element_type=jnp.float32)  12.8 us
  transfers between devices with their start and end apart: 6, of which 1 were waited for; matrix products, arithmetic and copies ran while one was open for 10% of the time, Pallas kernels for 0%

profile of v1, /device:TPU:0, one launch (start us, length us, event | category | flops | bytes accessed | tf_op | source)
XLA Modules:
  0.0 425.3 jit_solution(8674074670416610129)
XLA Ops:
  8.4 5.0 %collective-permute-start = (bf16[1,1,2,2,8,16,768]{6,5,4,3,2,1,0:T(8,128)(2,1)S(1)}, bf16[1,1,2,2,8,16,768]{6,5,4,3,2,1,0:T(8,128)(2,1)S(1)}, u32[]{:S(2)}, u32[]{:S(2)}) collective-permute-start(bf16[1,1,2,2,8,16,768]{6,5,4,3,2,1,0:T(8,128)(2,1)S(1)} %maximum_bitcast_fusion.1), channel_id=1, source_target_pairs={{0,4},{4,8},{8,12},{1,5},{5,9},{9,13},{2,6},{6,10},{10,14},{3,7},{... | collective-permute-start | bytes 2359304 | tf_op jit(solution)/shard_map/ppermute | solution.py:16
  14.7 29.3 %while.46 = (s32[]{:T(128)}, f32[6,128]{1,0:T(8,128)S(1)}, f32[6,128]{1,0:T(8,128)S(1)}, f32[6,128,128]{1,2,0:T(8,128)S(1)}, s32[6]{0:T(128)S(1)}, /*index=5*/bf...) while((s32[]{:T(128)}, f32[6,128]{1,0:T(8,128)S(1)}, ...), condition=%wide.region_8.9_spmd, body=%wide.region_5.0_spmd.sunk | while | flops 25542404 | bytes 1218243 | solution.py:45
  44.0 22.7 %pmax.7 = f32[128,6]{0,1:T(8,128)S(1)} all-reduce(f32[128,6]{0,1:T(8,128)S(1)} %bitcast.239), channel_id=1, replica_groups=mesh['group'=2,'frame'=4,'row'=2,'head'=2] {'frame','row'}, use_global_device_ids=true, to_apply=%region_9.10 | all-reduce | flops 768 | bytes 6144 | tf_op jit(solution)/shard_map/pmax | solution.py:100
  68.6 1.7 pad_maximum_fusion
  70.3 2.8 collective-permute-start.2
  74.4 17.6 %while.47 = (s32[]{:T(128)}, f32[6,16]{1,0:T(8,128)S(1)}, f32[6,16]{1,0:T(8,128)S(1)}, f32[6,16,128]{2,1,0:T(8,128)S(1)}, s32[6]{0:T(128)S(1)}, /*index=5*/bf16[...) while((s32[]{:T(128)}, f32[6,16]{1,0:T(8,128)S(1)}, ...), condition=%wide.region_15.16_spmd, body=%wide.region_12.15_spmd.sunk | while | flops 1597414 | bytes 162435 | solution.py:45
  92.0 39.7 %psum.30 = f32[128,6]{0,1:T(8,128)S(1)} all-reduce(f32[128,6]{0,1:T(8,128)S(1)} %get-tuple-element.582), channel_id=1, replica_groups=mesh['group'=2,'frame'=4,'row'=2,'head'=2] {'row'}, use_global_device_ids=true, to_apply=%region_16.17 | all-reduce | flops 768 | bytes 6144 | tf_op jit(solution)/shard_map/psum | solution.py:103
  131.7 10.1 %psum.31 = f32[128,6]{0,1:T(8,128)S(1)} all-reduce(f32[128,6]{0,1:T(8,128)S(1)} %psum.30), channel_id=1, replica_groups=mesh['group'=2,'frame'=4,'row'=2,'head'=2] {'frame'}, use_global_device_ids=true, to_apply=%region_17.18 | all-reduce | flops 768 | bytes 6144 | tf_op jit(solution)/shard_map/psum | solution.py:102
  142.3 34.3 %all-reduce.6.cloned.1.call-done = f32[128,768]{1,0:T(8,128)} async-done(((f32[128,768]{1,0:T(8,128)}), f32[128,768]{1,0:T(8,128)}) %all-reduce.6.cloned.1.call-update) | async-done | bytes 393232 | tf_op jit(solution)/shard_map/psum | solution.py:102
  176.8 1.5 fusion.61
  178.3 5.9 %maximum_bitcast_fusion = bf16[3,3,2,2,8,2,8,768]{7,6,5,4,3,2,1,0:T(8,128)(2,1)} fusion(bf16[3,1,2,2,8,16,768]{6,5,4,3,2,1,0:T(8,128)(2,1)} %collective-permute-done.3, bf16[1,1,2,2,8,16,768]{6,5,4,3,2,1,0:T(8,128)(2,1)S(1)} %collective-permute-done.1, bf16[1,1,2,2,8,16,768]{6,5,4,3,2,1,0:T(8,128)(2,1)S(1)} %maximum_bitcast_fusion.1, ...), kind=kLoop, calls=%fused_computation.100 | loop fusion | flops 14155776 | bytes 14155776 | tf_op jit(solution)/shard_map/reshape | solution.py:112
  184.2 233.4 %while.48 = (s32[]{:T(128)}, bf16[12,128,128]{2,1,0:T(8,128)(2,1)S(1)}, s32[12]{0:T(128)S(1)}, s32[2,27]{1,0:T(2,128)S(1)}, bf16[2,128,768]{2,1,0:T(8,128)(2,1)S...) while((s32[]{:T(128)}, ...), condition=%wide.region_4.5_spmd.clone, body=%wide.region_0.4_spmd.clone.sunk | while | flops 164492608 | bytes 10002113 | solution.py:187
  188.2 4.7 %select_reduce_fusion.2 = (pred[2304]{0:T(1024)(128)(4,1)S(1)}, pred[2304]{0:T(1024)(128)(4,1)S(1)}, pred[2304]{0:T(1024)(128)(4,1)S(1)}, pred[2304]{0:T(1024)(1...) fusion(pred[]{:T(512)} %bitcast.204, ...), kind=kLoop, calls=%fused_computation.55.clone.1 | loop fusion | flops 57600 | bytes 46087 | tf_op jit(solution)/shard_map/while/body/eval_jaxpr/jit(_take)/gather | solution.py:159
  192.9 7.0 %fusion.121 = pred[2304]{0:T(1024)(128)(4,1)S(1)} fusion(pred[2304]{0:T(1024)(128)(4,1)S(1)} %get-tuple-element.846, pred[2304]{0:T(1024)(128)(4,1)S(1)} %get-tuple-element.847, pred[2304]{0:T(1024)(128)(4,1)S(1)} %get-tuple-element.848, pred[2304]{0:T(1024)(128)(4,1)S(1)} %get-tuple-element.849, pred[2304]{0:T(1024)(128)(4,1)S(1)} %get-tuple-element.850, ...), kind=kLoop, calls=%fused_computation.79.clone.1 | loop fusion | flops 46080 | bytes 29963 | tf_op jit(solution)/shard_map/while/body/eval_jaxpr/jit(_take)/select_n | solution.py:159
  200.7 1.6 copy_bitcast_fusion.3
  207.7 4.7 %select_reduce_fusion.2 = (pred[2304]{0:T(1024)(128)(4,1)S(1)}, pred[2304]{0:T(1024)(128)(4,1)S(1)}, pred[2304]{0:T(1024)(128)(4,1)S(1)}, pred[2304]{0:T(1024)(1...) fusion(pred[]{:T(512)} %bitcast.204, ...), kind=kLoop, calls=%fused_computation.55.clone.1 | loop fusion | flops 57600 | bytes 46087 | tf_op jit(solution)/shard_map/while/body/eval_jaxpr/jit(_take)/gather | solution.py:159
  212.4 7.0 %fusion.121 = pred[2304]{0:T(1024)(128)(4,1)S(1)} fusion(pred[2304]{0:T(1024)(128)(4,1)S(1)} %get-tuple-element.846, pred[2304]{0:T(1024)(128)(4,1)S(1)} %get-tuple-element.847, pred[2304]{0:T(1024)(128)(4,1)S(1)} %get-tuple-element.848, pred[2304]{0:T(1024)(128)(4,1)S(1)} %get-tuple-element.849, pred[2304]{0:T(1024)(128)(4,1)S(1)} %get-tuple-element.850, ...), kind=kLoop, calls=%fused_computation.79.clone.1 | loop fusion | flops 46080 | bytes 29963 | tf_op jit(solution)/shard_map/while/body/eval_jaxpr/jit(_take)/select_n | solution.py:159
  220.2 1.6 copy_bitcast_fusion.3
  227.1 4.7 %select_reduce_fusion.2 = (pred[2304]{0:T(1024)(128)(4,1)S(1)}, pred[2304]{0:T(1024)(128)(4,1)S(1)}, pred[2304]{0:T(1024)(128)(4,1)S(1)}, pred[2304]{0:T(1024)(1...) fusion(pred[]{:T(512)} %bitcast.204, ...), kind=kLoop, calls=%fused_computation.55.clone.1 | loop fusion | flops 57600 | bytes 46087 | tf_op jit(solution)/shard_map/while/body/eval_jaxpr/jit(_take)/gather | solution.py:159
  231.8 7.0 %fusion.121 = pred[2304]{0:T(1024)(128)(4,1)S(1)} fusion(pred[2304]{0:T(1024)(128)(4,1)S(1)} %get-tuple-element.846, pred[2304]{0:T(1024)(128)(4,1)S(1)} %get-tuple-element.847, pred[2304]{0:T(1024)(128)(4,1)S(1)} %get-tuple-element.848, pred[2304]{0:T(1024)(128)(4,1)S(1)} %get-tuple-element.849, pred[2304]{0:T(1024)(128)(4,1)S(1)} %get-tuple-element.850, ...), kind=kLoop, calls=%fused_computation.79.clone.1 | loop fusion | flops 46080 | bytes 29963 | tf_op jit(solution)/shard_map/while/body/eval_jaxpr/jit(_take)/select_n | solution.py:159
  239.6 1.6 copy_bitcast_fusion.3
  246.6 4.7 %select_reduce_fusion.2 = (pred[2304]{0:T(1024)(128)(4,1)S(1)}, pred[2304]{0:T(1024)(128)(4,1)S(1)}, pred[2304]{0:T(1024)(128)(4,1)S(1)}, pred[2304]{0:T(1024)(1...) fusion(pred[]{:T(512)} %bitcast.204, ...), kind=kLoop, calls=%fused_computation.55.clone.1 | loop fusion | flops 57600 | bytes 46087 | tf_op jit(solution)/shard_map/while/body/eval_jaxpr/jit(_take)/gather | solution.py:159
  251.3 7.0 %fusion.121 = pred[2304]{0:T(1024)(128)(4,1)S(1)} fusion(pred[2304]{0:T(1024)(128)(4,1)S(1)} %get-tuple-element.846, pred[2304]{0:T(1024)(128)(4,1)S(1)} %get-tuple-element.847, pred[2304]{0:T(1024)(128)(4,1)S(1)} %get-tuple-element.848, pred[2304]{0:T(1024)(128)(4,1)S(1)} %get-tuple-element.849, pred[2304]{0:T(1024)(128)(4,1)S(1)} %get-tuple-element.850, ...), kind=kLoop, calls=%fused_computation.79.clone.1 | loop fusion | flops 46080 | bytes 29963 | tf_op jit(solution)/shard_map/while/body/eval_jaxpr/jit(_take)/select_n | solution.py:159
  259.1 1.6 copy_bitcast_fusion.3
  266.0 4.7 %select_reduce_fusion.2 = (pred[2304]{0:T(1024)(128)(4,1)S(1)}, pred[2304]{0:T(1024)(128)(4,1)S(1)}, pred[2304]{0:T(1024)(128)(4,1)S(1)}, pred[2304]{0:T(1024)(1...) fusion(pred[]{:T(512)} %bitcast.204, ...), kind=kLoop, calls=%fused_computation.55.clone.1 | loop fusion | flops 57600 | bytes 46087 | tf_op jit(solution)/shard_map/while/body/eval_jaxpr/jit(_take)/gather | solution.py:159
  270.7 7.0 %fusion.121 = pred[2304]{0:T(1024)(128)(4,1)S(1)} fusion(pred[2304]{0:T(1024)(128)(4,1)S(1)} %get-tuple-element.846, pred[2304]{0:T(1024)(128)(4,1)S(1)} %get-tuple-element.847, pred[2304]{0:T(1024)(128)(4,1)S(1)} %get-tuple-element.848, pred[2304]{0:T(1024)(128)(4,1)S(1)} %get-tuple-element.849, pred[2304]{0:T(1024)(128)(4,1)S(1)} %get-tuple-element.850, ...), kind=kLoop, calls=%fused_computation.79.clone.1 | loop fusion | flops 46080 | bytes 29963 | tf_op jit(solution)/shard_map/while/body/eval_jaxpr/jit(_take)/select_n | solution.py:159
  278.6 1.6 copy_bitcast_fusion.3
  285.5 4.7 %select_reduce_fusion.2 = (pred[2304]{0:T(1024)(128)(4,1)S(1)}, pred[2304]{0:T(1024)(128)(4,1)S(1)}, pred[2304]{0:T(1024)(128)(4,1)S(1)}, pred[2304]{0:T(1024)(1...) fusion(pred[]{:T(512)} %bitcast.204, ...), kind=kLoop, calls=%fused_computation.55.clone.1 | loop fusion | flops 57600 | bytes 46087 | tf_op jit(solution)/shard_map/while/body/eval_jaxpr/jit(_take)/gather | solution.py:159
  290.2 7.0 %fusion.121 = pred[2304]{0:T(1024)(128)(4,1)S(1)} fusion(pred[2304]{0:T(1024)(128)(4,1)S(1)} %get-tuple-element.846, pred[2304]{0:T(1024)(128)(4,1)S(1)} %get-tuple-element.847, pred[2304]{0:T(1024)(128)(4,1)S(1)} %get-tuple-element.848, pred[2304]{0:T(1024)(128)(4,1)S(1)} %get-tuple-element.849, pred[2304]{0:T(1024)(128)(4,1)S(1)} %get-tuple-element.850, ...), kind=kLoop, calls=%fused_computation.79.clone.1 | loop fusion | flops 46080 | bytes 29963 | tf_op jit(solution)/shard_map/while/body/eval_jaxpr/jit(_take)/select_n | solution.py:159
  298.0 1.6 copy_bitcast_fusion.3
  304.9 4.7 %select_reduce_fusion.2 = (pred[2304]{0:T(1024)(128)(4,1)S(1)}, pred[2304]{0:T(1024)(128)(4,1)S(1)}, pred[2304]{0:T(1024)(128)(4,1)S(1)}, pred[2304]{0:T(1024)(1...) fusion(pred[]{:T(512)} %bitcast.204, ...), kind=kLoop, calls=%fused_computation.55.clone.1 | loop fusion | flops 57600 | bytes 46087 | tf_op jit(solution)/shard_map/while/body/eval_jaxpr/jit(_take)/gather | solution.py:159
  309.6 7.0 %fusion.121 = pred[2304]{0:T(1024)(128)(4,1)S(1)} fusion(pred[2304]{0:T(1024)(128)(4,1)S(1)} %get-tuple-element.846, pred[2304]{0:T(1024)(128)(4,1)S(1)} %get-tuple-element.847, pred[2304]{0:T(1024)(128)(4,1)S(1)} %get-tuple-element.848, pred[2304]{0:T(1024)(128)(4,1)S(1)} %get-tuple-element.849, pred[2304]{0:T(1024)(128)(4,1)S(1)} %get-tuple-element.850, ...), kind=kLoop, calls=%fused_computation.79.clone.1 | loop fusion | flops 46080 | bytes 29963 | tf_op jit(solution)/shard_map/while/body/eval_jaxpr/jit(_take)/select_n | solution.py:159
  317.5 1.6 copy_bitcast_fusion.3
  324.4 4.7 %select_reduce_fusion.2 = (pred[2304]{0:T(1024)(128)(4,1)S(1)}, pred[2304]{0:T(1024)(128)(4,1)S(1)}, pred[2304]{0:T(1024)(128)(4,1)S(1)}, pred[2304]{0:T(1024)(1...) fusion(pred[]{:T(512)} %bitcast.204, ...), kind=kLoop, calls=%fused_computation.55.clone.1 | loop fusion | flops 57600 | bytes 46087 | tf_op jit(solution)/shard_map/while/body/eval_jaxpr/jit(_take)/gather | solution.py:159
  329.1 7.0 %fusion.121 = pred[2304]{0:T(1024)(128)(4,1)S(1)} fusion(pred[2304]{0:T(1024)(128)(4,1)S(1)} %get-tuple-element.846, pred[2304]{0:T(1024)(128)(4,1)S(1)} %get-tuple-element.847, pred[2304]{0:T(1024)(128)(4,1)S(1)} %get-tuple-element.848, pred[2304]{0:T(1024)(128)(4,1)S(1)} %get-tuple-element.849, pred[2304]{0:T(1024)(128)(4,1)S(1)} %get-tuple-element.850, ...), kind=kLoop, calls=%fused_computation.79.clone.1 | loop fusion | flops 46080 | bytes 29963 | tf_op jit(solution)/shard_map/while/body/eval_jaxpr/jit(_take)/select_n | solution.py:159
  336.9 1.6 copy_bitcast_fusion.3
  343.8 4.7 %select_reduce_fusion.2 = (pred[2304]{0:T(1024)(128)(4,1)S(1)}, pred[2304]{0:T(1024)(128)(4,1)S(1)}, pred[2304]{0:T(1024)(128)(4,1)S(1)}, pred[2304]{0:T(1024)(1...) fusion(pred[]{:T(512)} %bitcast.204, ...), kind=kLoop, calls=%fused_computation.55.clone.1 | loop fusion | flops 57600 | bytes 46087 | tf_op jit(solution)/shard_map/while/body/eval_jaxpr/jit(_take)/gather | solution.py:159
  348.5 7.0 %fusion.121 = pred[2304]{0:T(1024)(128)(4,1)S(1)} fusion(pred[2304]{0:T(1024)(128)(4,1)S(1)} %get-tuple-element.846, pred[2304]{0:T(1024)(128)(4,1)S(1)} %get-tuple-element.847, pred[2304]{0:T(1024)(128)(4,1)S(1)} %get-tuple-element.848, pred[2304]{0:T(1024)(128)(4,1)S(1)} %get-tuple-element.849, pred[2304]{0:T(1024)(128)(4,1)S(1)} %get-tuple-element.850, ...), kind=kLoop, calls=%fused_computation.79.clone.1 | loop fusion | flops 46080 | bytes 29963 | tf_op jit(solution)/shard_map/while/body/eval_jaxpr/jit(_take)/select_n | solution.py:159
  356.4 1.6 copy_bitcast_fusion.3
  363.3 4.7 %select_reduce_fusion.2 = (pred[2304]{0:T(1024)(128)(4,1)S(1)}, pred[2304]{0:T(1024)(128)(4,1)S(1)}, pred[2304]{0:T(1024)(128)(4,1)S(1)}, pred[2304]{0:T(1024)(1...) fusion(pred[]{:T(512)} %bitcast.204, ...), kind=kLoop, calls=%fused_computation.55.clone.1 | loop fusion | flops 57600 | bytes 46087 | tf_op jit(solution)/shard_map/while/body/eval_jaxpr/jit(_take)/gather | solution.py:159
  368.0 7.0 %fusion.121 = pred[2304]{0:T(1024)(128)(4,1)S(1)} fusion(pred[2304]{0:T(1024)(128)(4,1)S(1)} %get-tuple-element.846, pred[2304]{0:T(1024)(128)(4,1)S(1)} %get-tuple-element.847, pred[2304]{0:T(1024)(128)(4,1)S(1)} %get-tuple-element.848, pred[2304]{0:T(1024)(128)(4,1)S(1)} %get-tuple-element.849, pred[2304]{0:T(1024)(128)(4,1)S(1)} %get-tuple-element.850, ...), kind=kLoop, calls=%fused_computation.79.clone.1 | loop fusion | flops 46080 | bytes 29963 | tf_op jit(solution)/shard_map/while/body/eval_jaxpr/jit(_take)/select_n | solution.py:159
  375.8 1.6 copy_bitcast_fusion.3
  382.7 4.7 %select_reduce_fusion.2 = (pred[2304]{0:T(1024)(128)(4,1)S(1)}, pred[2304]{0:T(1024)(128)(4,1)S(1)}, pred[2304]{0:T(1024)(128)(4,1)S(1)}, pred[2304]{0:T(1024)(1...) fusion(pred[]{:T(512)} %bitcast.204, ...), kind=kLoop, calls=%fused_computation.55.clone.1 | loop fusion | flops 57600 | bytes 46087 | tf_op jit(solution)/shard_map/while/body/eval_jaxpr/jit(_take)/gather | solution.py:159
  387.4 7.0 %fusion.121 = pred[2304]{0:T(1024)(128)(4,1)S(1)} fusion(pred[2304]{0:T(1024)(128)(4,1)S(1)} %get-tuple-element.846, pred[2304]{0:T(1024)(128)(4,1)S(1)} %get-tuple-element.847, pred[2304]{0:T(1024)(128)(4,1)S(1)} %get-tuple-element.848, pred[2304]{0:T(1024)(128)(4,1)S(1)} %get-tuple-element.849, pred[2304]{0:T(1024)(128)(4,1)S(1)} %get-tuple-element.850, ...), kind=kLoop, calls=%fused_computation.79.clone.1 | loop fusion | flops 46080 | bytes 29963 | tf_op jit(solution)/shard_map/while/body/eval_jaxpr/jit(_take)/select_n | solution.py:159
  395.3 1.6 copy_bitcast_fusion.3
  402.2 4.7 %select_reduce_fusion.2 = (pred[2304]{0:T(1024)(128)(4,1)S(1)}, pred[2304]{0:T(1024)(128)(4,1)S(1)}, pred[2304]{0:T(1024)(128)(4,1)S(1)}, pred[2304]{0:T(1024)(1...) fusion(pred[]{:T(512)} %bitcast.204, ...), kind=kLoop, calls=%fused_computation.55.clone.1 | loop fusion | flops 57600 | bytes 46087 | tf_op jit(solution)/shard_map/while/body/eval_jaxpr/jit(_take)/gather | solution.py:159
  406.9 7.0 %fusion.121 = pred[2304]{0:T(1024)(128)(4,1)S(1)} fusion(pred[2304]{0:T(1024)(128)(4,1)S(1)} %get-tuple-element.846, pred[2304]{0:T(1024)(128)(4,1)S(1)} %get-tuple-element.847, pred[2304]{0:T(1024)(128)(4,1)S(1)} %get-tuple-element.848, pred[2304]{0:T(1024)(128)(4,1)S(1)} %get-tuple-element.849, pred[2304]{0:T(1024)(128)(4,1)S(1)} %get-tuple-element.850, ...), kind=kLoop, calls=%fused_computation.79.clone.1 | loop fusion | flops 46080 | bytes 29963 | tf_op jit(solution)/shard_map/while/body/eval_jaxpr/jit(_take)/select_n | solution.py:159
  414.7 1.6 copy_bitcast_fusion.3
  (368 shorter events, 94.8 us)
Async XLA Ops:
  7.2 135.0 %all-reduce.4.cloned.1.call-start = ((), (), s32[]{:S(2)}) async-start(), calls=%async_computation | async-start | bytes 786432 | tf_op jit(solution)/shard_map/psum | solution.py:103
  8.4 60.2 %collective-permute-start = (bf16[1,1,2,2,8,16,768]{6,5,4,3,2,1,0:T(8,128)(2,1)S(1)}, bf16[1,1,2,2,8,16,768]{6,5,4,3,2,1,0:T(8,128)(2,1)S(1)}, u32[]{:S(2)}, u32[]{:S(2)}) collective-permute-start(bf16[1,1,2,2,8,16,768]{6,5,4,3,2,1,0:T(8,128)(2,1)S(1)} %maximum_bitcast_fusion.1), channel_id=1, source_target_pairs={{0,4},{4,8},{8,12},{1,5},{5,9},{9,13},{2,6},{6,10},{10,14},{3,7},{... | collective-permute-start | bytes 2359304 | tf_op jit(solution)/shard_map/ppermute | solution.py:16
  13.4 55.2 %collective-permute-start.1 = (bf16[1,1,2,2,8,16,768]{6,5,4,3,2,1,0:T(8,128)(2,1)S(1)}, bf16[1,1,2,2,8,16,768]{6,5,4,3,2,1,0:T(8,128)(2,1)S(1)}, u32[]{:S(2)}, u32[]{:S(2)}) collective-permute-start(bf16[1,1,2,2,8,16,768]{6,5,4,3,2,1,0:T(8,128)(2,1)S(1)} %maximum_bitcast_fusion.1), channel_id=1, source_target_pairs={{4,0},{8,4},{12,8},{5,1},{9,5},{13,9},{6,2},{10,6},{14,10},{7,3},{... | collective-permute-start | bytes 2359304 | tf_op jit(solution)/shard_map/ppermute | solution.py:17
  67.8 108.9 %all-reduce.6.cloned.1.call-start = ((), (), s32[]{:S(2)}) async-start(), calls=%async_computation.1 | async-start | bytes 786432 | tf_op jit(solution)/shard_map/psum | solution.py:102
  68.6 5.8 %copy-start.2 = (bf16[128,768]{1,0:T(8,128)(2,1)S(1)}, bf16[128,768]{1,0:T(8,128)(2,1)}, u32[]{:S(2)}) copy-start(bf16[128,768]{1,0:T(8,128)(2,1)} %param.20) | copy-start | bytes 589828
  68.6 73.5 %copy-start = (bf16[2,8,16,768]{3,2,1,0:T(8,128)(2,1)S(1)}, bf16[2,8,16,768]{3,2,1,0:T(8,128)(2,1)}, u32[]{:S(2)}) copy-start(bf16[2,8,16,768]{3,2,1,0:T(8,128)(2,1)} %param.15) | copy-start | bytes 1179652
  70.3 71.9 %copy-start.3 = (s32[1,1,2,26]{3,2,1,0:T(2,128)S(1)}, s32[1,1,2,26]{3,2,1,0:T(2,128)}, u32[]{:S(2)}) copy-start(s32[1,1,2,26]{3,2,1,0:T(2,128)} %param.21) | copy-start | bytes 628
  70.3 108.0 %collective-permute-start.2 = (bf16[3,1,2,2,8,16,768]{6,5,4,3,2,1,0:T(8,128)(2,1)}, bf16[3,1,2,2,8,16,768]{6,5,4,3,2,1,0:T(8,128)(2,1)}, u32[]{:S(2)}, u32[]{:S(2)}) collective-permute-start(bf16[3,1,2,2,8,16,768]{6,5,4,3,2,1,0:T(8,128)(2,1)} %pad_maximum_fusion), channel_id=1, source_target_pairs={{0,2},{1,3},{4,6},{5,7},{8,10},{9,11},{12,14},{13,15},{16,18},{17,... | collective-permute-start | bytes 7077896 | tf_op jit(solution)/shard_map/ppermute | solution.py:16
  73.1 105.2 %collective-permute-start.3 = (bf16[3,1,2,2,8,16,768]{6,5,4,3,2,1,0:T(8,128)(2,1)}, bf16[3,1,2,2,8,16,768]{6,5,4,3,2,1,0:T(8,128)(2,1)}, u32[]{:S(2)}, u32[]{:S(2)}) collective-permute-start(bf16[3,1,2,2,8,16,768]{6,5,4,3,2,1,0:T(8,128)(2,1)} %pad_maximum_fusion), channel_id=1, source_target_pairs={{2,0},{3,1},{6,4},{7,5},{10,8},{11,9},{14,12},{15,13},{18,16},{19,... | collective-permute-start | bytes 7077896 | tf_op jit(solution)/shard_map/ppermute | solution.py:17
  178.3 5.9 %copy-start.1 = (bf16[12,128,128]{2,1,0:T(8,128)(2,1)S(1)}, bf16[12,128,128]{2,1,0:T(8,128)(2,1)}, u32[]{:S(2)}) copy-start(bf16[12,128,128]{2,1,0:T(8,128)(2,1)} %custom-call.6) | copy-start | bytes 1179652
Sparse Core Ops, SparseCore 0:
  67.9 31.7 all-reduce.3
  142.3 34.2 all-reduce.5
